TPU v7x, 32 devices: a whole 2x2x4 slice. The times are simulated.
32 devices in a mesh: chain: 2 (over y), cell: 4 (over z), col: 4 (over x, core).
Axes of the slice: x: 2, y: 2, z: 4, core: 2. Of those that a mesh axis runs over, the one named last changes fastest.
Arguments:
- grad: float32 [16384, 64], P(('chain', 'cell', 'col')), parts along dimension 0, may hold values from -6 to 6
- near_tiles: bfloat16 [4, 2, 2048, 2048], P('cell', None, 'col'), may hold values from -0.09375 to 0.09375
- tile_count: int32 [4], replicated, may hold values from 1 to 2
- near_offset: int32 [4], replicated, may hold values from -2 to 2, as said below
- far_src: int32 [4, 8], replicated, may hold values from 0 to 3
- far_count: int32 [4], replicated, may hold values from 1 to 8
- far_cores: float32 [4, 8, 64, 64], P('cell'), may hold values from -0.25 to 0.25
- basis_out: bfloat16 [8192, 64], P(('cell', 'col')), may hold values from -0.75 to 0.75
- basis_in: bfloat16 [8192, 64], P(('cell', 'col')), may hold values from -0.125 to 0.125
Outputs:
- step_block: float32 [16384, 64], P(('chain', 'cell', 'col')), parts along dimension 0
There are 2 independent parts, one for each index of `chain`. A program takes and returns all parts, laid end to end along the dimension named above; an argument that names none is the same for every part. Nothing has to cross between parts.
Inputs may be any that keep to these rules, and one draw needn't show every extreme that they name: c + near_offset[c] is a cluster of the chain, and near_offset[c] is never 0.
All inputs are finite; a program needn't handle non-finite values.
Results may differ from a plain program's by a relative error of at most 0.0035.
Values may be sent and summed in bfloat16 or wider, within the bound.
No kernel may reach another device: no remote copies, remote signals or barrier semaphores. Data moves between devices by JAX's collectives and lax.ppermute only.
A program may use at most 64 MiB of HBM per device.

v0:
```python
import jax
import jax.numpy as jnp
from jax import lax
from jax.sharding import PartitionSpec as P


def shifted(value, axis, by):
    devices = lax.axis_size(axis)
    pairs = [(i, i + by) for i in range(devices) if 0 <= i + by < devices]
    return lax.ppermute(value, axis, pairs)


def pick_offset(stacked, offset):
    position = offset + 2 - (offset > 0).astype(jnp.int32)
    return lax.dynamic_index_in_dim(stacked, position, 0, keepdims=False)


def coupling(table, sources, count, cores):
    picked = jnp.take(table, sources, axis=0)
    slots = jnp.arange(cores.shape[0], dtype=jnp.int32)
    masked = jnp.where((slots < count)[:, None, None], cores, jnp.zeros_like(cores))
    return jnp.einsum("kab,kbw->aw", masked, picked, precision=lax.Precision.HIGHEST)


def body(
    grad, near_tiles, tile_count, near_offset, far_src, far_count, far_cores, basis_out, basis_in
):
    owner = lax.axis_index("cell")
    rounded = grad.astype(jnp.bfloat16)
    offset = near_offset[owner]
    steps_list = (-2, -1, 1, 2)
    whole = lax.all_gather(rounded, "col", axis=0, tiled=True)
    moved = [shifted(whole, "cell", -step) for step in steps_list]
    beside = pick_offset(jnp.stack(moved), offset)
    tiles = near_tiles[0]
    own_term = jnp.dot(tiles[0], whole, preferred_element_type=jnp.float32)
    other_term = jnp.dot(tiles[1], beside, preferred_element_type=jnp.float32)
    near = own_term + jnp.where(tile_count[owner] == 2, other_term, jnp.zeros_like(other_term))
    partial_proj = lax.dot_general(
        basis_in, rounded, (((0,), (0,)), ((), ())), preferred_element_type=jnp.float32
    )
    sources = far_src[owner]
    count = far_count[owner]
    cores = far_cores[0]
    proj = lax.psum(partial_proj, "col")
    table = lax.all_gather(proj[None], "cell", axis=0, tiled=True)
    core_block = coupling(table, sources, count, cores).astype(jnp.bfloat16)
    far = jnp.dot(basis_out, core_block, preferred_element_type=jnp.float32)
    return near + far


def solution(mesh):
    placed = (
        P(("chain", "cell", "col"), None),
        P("cell", None, "col", None),
        P(),
        P(),
        P(),
        P(),
        P("cell", None, None, None),
        P(("cell", "col"), None),
        P(("cell", "col"), None),
    )
    return jax.shard_map(
        body,
        mesh=mesh,
        in_specs=placed,
        out_specs=P(("chain", "cell", "col"), None),
        check_vma=False,
    )
```

profile of v0, /device:TPU:0, one launch (start us, length us, event | category | flops | bytes accessed | tf_op | source)
XLA Modules:
  0.0 60.8 jit_solution(2780922674257491303)
XLA Ops:
  0.0 0.0 copy-start
  0.0 0.9 %convert_element_type.10 = bf16[512,64]{0,1:T(8,128)(2,1)S(1)} convert(f32[512,64]{0,1:T(8,128)} %param.9) | non-fusion elementwise | flops 32768 | bytes 196608 | tf_op jit(solution)/shard_map/convert_element_type | solution.py:29
  1.0 7.2 %all_gather.6 = bf16[2048,64]{0,1:T(8,128)(2,1)S(1)} all-gather(bf16[512,64]{0,1:T(8,128)(2,1)S(1)} %convert_element_type.10), channel_id=1, replica_groups=mesh['chain'=2,'cell'=4,'col'=4] {'col'}, dimensions={0}, use_global_device_ids=true | all-gather | bytes 327680 | tf_op jit(solution)/shard_map/all_gather | solution.py:32
  8.2 4.5 %collective-permute-start = (bf16[2048,64]{0,1:T(8,128)(2,1)S(1)}, bf16[2048,64]{0,1:T(8,128)(2,1)S(1)}, u32[]{:S(2)}, u32[]{:S(2)}) collective-permute-start(bf16[2048,64]{0,1:T(8,128)(2,1)S(1)} %all_gather.6), channel_id=1, source_target_pairs={{0,8},{4,12},{1,9},{5,13},{2,10},{6,14},{3,11},{7,15},{16,24},{20,... | collective-permute-start | bytes 786440 | tf_op jit(solution)/shard_map/ppermute | solution.py:10
  12.7 3.5 %collective-permute-start.1 = (bf16[2048,64]{0,1:T(8,128)(2,1)S(1)}, bf16[2048,64]{0,1:T(8,128)(2,1)S(1)}, u32[]{:S(2)}, u32[]{:S(2)}) collective-permute-start(bf16[2048,64]{0,1:T(8,128)(2,1)S(1)} %all_gather.6), channel_id=1, source_target_pairs={{0,4},{4,8},{8,12},{1,5},{5,9},{9,13},{2,6},{6,10},{10,14},{3,7},{... | collective-permute-start | bytes 786440 | tf_op jit(solution)/shard_map/ppermute | solution.py:10
  16.2 1.3 %collective-permute-start.2 = (bf16[2048,64]{0,1:T(8,128)(2,1)S(1)}, bf16[2048,64]{0,1:T(8,128)(2,1)S(1)}, u32[]{:S(2)}, u32[]{:S(2)}) collective-permute-start(bf16[2048,64]{0,1:T(8,128)(2,1)S(1)} %all_gather.6), channel_id=1, source_target_pairs={{4,0},{8,4},{12,8},{5,1},{9,5},{13,9},{6,2},{10,6},{14,10},{7,3},{... | collective-permute-start | bytes 786440 | tf_op jit(solution)/shard_map/ppermute | solution.py:10
  17.5 1.3 %collective-permute-start.3 = (bf16[2048,64]{0,1:T(8,128)(2,1)S(1)}, bf16[2048,64]{0,1:T(8,128)(2,1)S(1)}, u32[]{:S(2)}, u32[]{:S(2)}) collective-permute-start(bf16[2048,64]{0,1:T(8,128)(2,1)S(1)} %all_gather.6), channel_id=1, source_target_pairs={{8,0},{12,4},{9,1},{13,5},{10,2},{14,6},{11,3},{15,7},{24,16},{28,... | collective-permute-start | bytes 786440 | tf_op jit(solution)/shard_map/ppermute | solution.py:10
  18.8 1.2 %dynamic_slice.19 = s32[1]{0:T(128)} dynamic-slice(s32[4]{0:T(128)} %param.14, s32[]{:T(128)S(6)} %select_n.45), dynamic_slice_sizes={1} | dynamic-slice | bytes 12 | tf_op jit(solution)/shard_map/dynamic_slice | solution.py:43
  20.1 0.7 %fusion.30 = s32[8]{0:T(128)S(1)} fusion(s32[4,8]{1,0:T(4,128)} %param.13, s32[]{:T(128)S(6)} %select_n.45), kind=kLoop, calls=%fused_computation.35 | loop fusion | flops 24 | bytes 68 | tf_op jit(solution)/shard_map/jit(_take)/jit(_where)/select_n | solution.py:19
  20.8 1.3 %compare_and_fusion = (pred[8]{0:T(512)(128)(4,1)S(1)}, pred[8]{0:T(512)(128)(4,1)S(1)}) fusion(s32[4,8]{1,0:T(4,128)} %param.13, s32[]{:T(128)S(6)} %select_n.45, s32[]{:T(128)} %bitcast.10), kind=kLoop, calls=%fused_computation.32 | loop fusion | flops 56 | bytes 56 | tf_op jit(solution)/shard_map/jit(_take)/and | solution.py:19
  22.1 1.0 %convolution_bitcast_fusion.1 = f32[1,64,64]{2,1,0:T(8,128)S(1)} fusion(bf16[512,64]{0,1:T(8,128)(2,1)} %param.17, bf16[512,64]{0,1:T(8,128)(2,1)S(1)} %convert_element_type.10), kind=kOutput, calls=%fused_computation.12 | convolution fusion | flops 4194304 | bytes 147456 | tf_op jit(solution)/shard_map/dot_general | solution.py:39
  23.1 11.4 %psum.7 = f32[1,64,64]{2,1,0:T(8,128)S(1)} all-reduce(f32[1,64,64]{2,1,0:T(8,128)S(1)} %convolution_bitcast_fusion.1), channel_id=1, replica_groups=mesh['chain'=2,'cell'=4,'col'=4] {'col'}, use_global_device_ids=true, to_apply=%region_0.1 | all-reduce | flops 4096 | bytes 32768 | tf_op jit(solution)/shard_map/psum | solution.py:45
  34.5 14.3 %all_gather.7 = f32[4,64,64]{2,1,0:T(8,128)S(1)} all-gather(f32[1,64,64]{2,1,0:T(8,128)S(1)} %psum.7), channel_id=1, replica_groups=mesh['chain'=2,'cell'=4,'col'=4] {'cell'}, dimensions={0}, use_global_device_ids=true | all-gather | bytes 81920 | tf_op jit(solution)/shard_map/all_gather | solution.py:46
  48.8 0.6 gather_fusion
  49.3 1.4 %fusion.18 = bf16[64,64]{1,0:T(8,128)(2,1)S(1)} fusion(f32[1,8,64,64]{3,2,1,0:T(8,128)} %param.15, f32[8,64,64]{2,1,0:T(8,128)S(1)} %gather_fusion, pred[8]{0:T(512)(128)(4,1)S(1)} %get-tuple-element.5, pred[8]{0:T(512)(128)(4,1)S(1)} %get-tuple-element.6), kind=kOutput, calls=%fused_computation.14 | convolution fusion | flops 25235456 | bytes 270352 | tf_op jit(solution)/shard_map/kab,kbw->aw/dot_general | solution.py:22
  50.8 1.2 %dynamic_slice.17 = s32[1]{0:T(128)} dynamic-slice(s32[4]{0:T(128)} %param.12, s32[]{:T(128)S(6)} %select_n.45), dynamic_slice_sizes={1} | dynamic-slice | bytes 12 | tf_op jit(solution)/shard_map/dynamic_slice | solution.py:30
  53.3 1.3 %dynamic_slice.16 = s32[1]{0:T(128)} dynamic-slice(s32[4]{0:T(128)} %param.11, s32[]{:T(128)S(6)} %select_n.45), dynamic_slice_sizes={1} | dynamic-slice | bytes 12 | tf_op jit(solution)/shard_map/dynamic_slice | solution.py:38
  55.2 0.2 convolution_bitcast_fusion
  55.4 0.0 collective-permute-done
  55.4 0.0 collective-permute-done.1
  55.4 0.0 collective-permute-done.2
  55.4 0.0 collective-permute-done.3
  55.4 2.4 %fusion.15 = f32[512,64]{0,1:T(8,128)S(1)} fusion(bf16[1,2,512,2048]{3,2,1,0:T(8,128)(2,1)} %param.10, s32[]{:T(128)S(6)} %select_n.47, bf16[1,2048,64]{1,2,0:T(8,128)(2,1)S(1)} %bitcast.48, bf16[1,2048,64]{1,2,0:T(8,128)(2,1)S(1)} %bitcast.49, bf16[1,2048,64]{1,2,0:T(8,128)(2,1)S(1)} %bitcast.50, bf16[1,2048,64]{1,2,0:T(8,128)(2,1)S(1)} %bitcast.51, ...), kind=kOutput, calls=%fused_computation.10 | convolution fusion | flops 134643712 | bytes 3277316 | tf_op jit(solution)/shard_map/dot_general | solution.py:37
  57.8 3.0 %fusion.9 = f32[512,64]{0,1:T(8,128)} fusion(f32[512,64]{0,1:T(8,128)S(1)} %convolution_bitcast_fusion, f32[512,64]{0,1:T(8,128)S(1)} %fusion.15, bf16[2048,64]{0,1:T(8,128)(2,1)S(1)} %all_gather.6, bf16[1,2,512,2048]{3,2,1,0:T(8,128)(2,1)} %param.10), kind=kOutput, calls=%fused_computation.8 | convolution fusion | flops 134283264 | bytes 2752512 | tf_op jit(solution)/shard_map/dot_general | solution.py:36
  (2 shorter events, 0.0 us)
Async XLA Ops:
  0.0 55.2 %copy-start = (bf16[512,64]{0,1:T(8,128)(2,1)S(1)}, bf16[512,64]{0,1:T(8,128)(2,1)}, u32[]{:S(2)}) copy-start(bf16[512,64]{0,1:T(8,128)(2,1)} %param.16) | copy-start | bytes 196612
  8.2 47.2 %collective-permute-start = (bf16[2048,64]{0,1:T(8,128)(2,1)S(1)}, bf16[2048,64]{0,1:T(8,128)(2,1)S(1)}, u32[]{:S(2)}, u32[]{:S(2)}) collective-permute-start(bf16[2048,64]{0,1:T(8,128)(2,1)S(1)} %all_gather.6), channel_id=1, source_target_pairs={{0,8},{4,12},{1,9},{5,13},{2,10},{6,14},{3,11},{7,15},{16,24},{20,... | collective-permute-start | bytes 786440 | tf_op jit(solution)/shard_map/ppermute | solution.py:10
  12.7 42.7 %collective-permute-start.1 = (bf16[2048,64]{0,1:T(8,128)(2,1)S(1)}, bf16[2048,64]{0,1:T(8,128)(2,1)S(1)}, u32[]{:S(2)}, u32[]{:S(2)}) collective-permute-start(bf16[2048,64]{0,1:T(8,128)(2,1)S(1)} %all_gather.6), channel_id=1, source_target_pairs={{0,4},{4,8},{8,12},{1,5},{5,9},{9,13},{2,6},{6,10},{10,14},{3,7},{... | collective-permute-start | bytes 786440 | tf_op jit(solution)/shard_map/ppermute | solution.py:10
  16.2 39.2 %collective-permute-start.2 = (bf16[2048,64]{0,1:T(8,128)(2,1)S(1)}, bf16[2048,64]{0,1:T(8,128)(2,1)S(1)}, u32[]{:S(2)}, u32[]{:S(2)}) collective-permute-start(bf16[2048,64]{0,1:T(8,128)(2,1)S(1)} %all_gather.6), channel_id=1, source_target_pairs={{4,0},{8,4},{12,8},{5,1},{9,5},{13,9},{6,2},{10,6},{14,10},{7,3},{... | collective-permute-start | bytes 786440 | tf_op jit(solution)/shard_map/ppermute | solution.py:10
  17.5 37.9 %collective-permute-start.3 = (bf16[2048,64]{0,1:T(8,128)(2,1)S(1)}, bf16[2048,64]{0,1:T(8,128)(2,1)S(1)}, u32[]{:S(2)}, u32[]{:S(2)}) collective-permute-start(bf16[2048,64]{0,1:T(8,128)(2,1)S(1)} %all_gather.6), channel_id=1, source_target_pairs={{8,0},{12,4},{9,1},{13,5},{10,2},{14,6},{11,3},{15,7},{24,16},{28,... | collective-permute-start | bytes 786440 | tf_op jit(solution)/shard_map/ppermute | solution.py:10
where the time goes:
time: 61.3 us; the launch traced here: 60.8 us
  blocking collectives  32.9 us (54%)
  starting transfers between devices  10.6 us (17%)
  matrix products  7.95 us (13%)
  local copies, waits for them, and re-layouts  4.33 us (7%)
  other arithmetic  2.98 us (5%)
  between operations  2.04 us (3%)
    all_gather x1, blocking collectives, body(): table = lax.all_gather(proj[None], 'cell', axis=0, tiled=True)  14.3 us
    psum x1, blocking collectives, body(): proj = lax.psum(partial_proj, 'col')  11.4 us
    ppermute x4, starting transfers between devices, shifted(): return lax.ppermute(value, axis, pairs)  10.6 us
    all_gather x1, blocking collectives, body(): whole = lax.all_gather(rounded, 'col', axis=0, tiled=True)  7.22 us
    dot_general x1, matrix products, body(): own_term = jnp.dot(tiles[0], whole, preferred_element_type=jnp.float32)  3.01 us
    dot_general x1, matrix products, body(): other_term = jnp.dot(tiles[1], beside, preferred_element_type=jnp.float32)  2.36 us
    dot_general x1, matrix products, coupling(): jnp.einsum('kab,kbw->aw', masked, picked, precision=lax.Precision.HIGHEST)  1.42 us
    and x1, other arithmetic, coupling(): picked = jnp.take(table, sources, axis=0)  1.34 us
  transfers between devices with their start and end apart: 4, of which 0 were waited for; matrix products, arithmetic and copies ran while one was open for 15% of the time, Pallas kernels for 0%

commit v1 on v0

--- a/solution.py
+++ b/solution.py
@@ -43,7 +43,9 @@
     count = far_count[owner]
     cores = far_cores[0]
     proj = lax.psum(partial_proj, "col")
-    table = lax.all_gather(proj[None], "cell", axis=0, tiled=True)
+    table = jnp.concatenate(
+        lax.all_to_all(jnp.stack([proj[None]] * lax.axis_size("cell")), "cell", 0, 0), axis=0
+    )
     core_block = coupling(table, sources, count, cores).astype(jnp.bfloat16)
     far = jnp.dot(basis_out, core_block, preferred_element_type=jnp.float32)
     return near + far

time: 61.3 us -> 53.7 us (0.88)
  blocking collectives: 32.9 us -> 18.6 us
  starting transfers between devices: 10.6 us -> 16.7 us
  matrix products: 7.95 us -> 6.52 us
  local copies, waits for them, and re-layouts: 4.33 us -> 5.72 us
  other arithmetic: 2.98 us -> 3.71 us
    all_gather x1 -> x0, blocking collectives: 14.3 us -> none  [body(): table = lax.all_gather(proj[None], 'cell', axis=0, tiled=True)]
    all_to_all x0 -> x1, starting transfers between devices: none -> 6.13 us  [body(): lax.all_to_all(jnp.stack([proj[None]] * lax.axis_size('cell')), 'cell', 0...]
    dot_general x1, matrix products: 3.01 us -> 1.44 us  [body(): own_term = jnp.dot(tiles[0], whole, preferred_element_type=jnp.float32)]
    unnamed x2 -> x6, local copies, waits for them, and re-layouts: 0.01 us -> 0.89 us
    all_to_all x0 -> x1, other arithmetic: none -> 0.81 us  [body(): lax.all_to_all(jnp.stack([proj[None]] * lax.axis_size('cell')), 'cell', 0...]
  transfers between devices with their start and end apart: 4 -> 5, of which waited for: 0 -> 0; matrix products, arithmetic and copies ran while one was open for 15% -> 21% of each run, Pallas kernels for 0% -> 0%
where the time goes in v1:
time: 53.7 us; the launch traced here: 53.2 us
  blocking collectives  18.6 us (35%)
  starting transfers between devices  16.7 us (31%)
  matrix products  6.52 us (12%)
  local copies, waits for them, and re-layouts  5.72 us (11%)
  other arithmetic  3.71 us (7%)
  between operations  1.93 us (4%)
    psum x1, blocking collectives, body(): proj = lax.psum(partial_proj, 'col')  11.4 us
    ppermute x4, starting transfers between devices, shifted(): return lax.ppermute(value, axis, pairs)  10.6 us
    all_gather x1, blocking collectives, body(): whole = lax.all_gather(rounded, 'col', axis=0, tiled=True)  7.22 us
    all_to_all x1, starting transfers between devices, body(): lax.all_to_all(jnp.stack([proj[None]] * lax.axis_size('cell')), 'cell', 0...  6.13 us
    dot_general x1, matrix products, body(): other_term = jnp.dot(tiles[1], beside, preferred_element_type=jnp.float32)  2.36 us
    dot_general x1, matrix products, coupling(): jnp.einsum('kab,kbw->aw', masked, picked, precision=lax.Precision.HIGHEST)  1.57 us
    dot_general x1, matrix products, body(): own_term = jnp.dot(tiles[0], whole, preferred_element_type=jnp.float32)  1.44 us
    dynamic_slice x1, local copies, waits for them, and re-layouts, body(): offset = near_offset[owner]  1.27 us
  transfers between devices with their start and end apart: 5, of which 0 were waited for; matrix products, arithmetic and copies ran while one was open for 21% of the time, Pallas kernels for 0%

profile of v1, /device:TPU:0, one launch (start us, length us, event | category | flops | bytes accessed | tf_op | source)
XLA Modules:
  0.0 53.2 jit_solution(8446998134752604842)
XLA Ops:
  0.0 0.9 %convert_element_type.10 = bf16[512,64]{0,1:T(8,128)(2,1)S(1)} convert(f32[512,64]{0,1:T(8,128)} %param.9) | non-fusion elementwise | flops 32768 | bytes 196608 | tf_op jit(solution)/shard_map/convert_element_type | solution.py:29
  1.0 7.2 %all_gather.3 = bf16[2048,64]{0,1:T(8,128)(2,1)S(1)} all-gather(bf16[512,64]{0,1:T(8,128)(2,1)S(1)} %convert_element_type.10), channel_id=1, replica_groups=mesh['chain'=2,'cell'=4,'col'=4] {'col'}, dimensions={0}, use_global_device_ids=true | all-gather | bytes 327680 | tf_op jit(solution)/shard_map/all_gather | solution.py:32
  8.2 4.5 %collective-permute-start = (bf16[2048,64]{0,1:T(8,128)(2,1)S(1)}, bf16[2048,64]{0,1:T(8,128)(2,1)S(1)}, u32[]{:S(2)}, u32[]{:S(2)}) collective-permute-start(bf16[2048,64]{0,1:T(8,128)(2,1)S(1)} %all_gather.3), channel_id=1, source_target_pairs={{0,8},{4,12},{1,9},{5,13},{2,10},{6,14},{3,11},{7,15},{16,24},{20,... | collective-permute-start | bytes 786440 | tf_op jit(solution)/shard_map/ppermute | solution.py:10
  12.7 3.5 %collective-permute-start.1 = (bf16[2048,64]{0,1:T(8,128)(2,1)S(1)}, bf16[2048,64]{0,1:T(8,128)(2,1)S(1)}, u32[]{:S(2)}, u32[]{:S(2)}) collective-permute-start(bf16[2048,64]{0,1:T(8,128)(2,1)S(1)} %all_gather.3), channel_id=1, source_target_pairs={{0,4},{4,8},{8,12},{1,5},{5,9},{9,13},{2,6},{6,10},{10,14},{3,7},{... | collective-permute-start | bytes 786440 | tf_op jit(solution)/shard_map/ppermute | solution.py:10
  16.2 1.3 %collective-permute-start.2 = (bf16[2048,64]{0,1:T(8,128)(2,1)S(1)}, bf16[2048,64]{0,1:T(8,128)(2,1)S(1)}, u32[]{:S(2)}, u32[]{:S(2)}) collective-permute-start(bf16[2048,64]{0,1:T(8,128)(2,1)S(1)} %all_gather.3), channel_id=1, source_target_pairs={{4,0},{8,4},{12,8},{5,1},{9,5},{13,9},{6,2},{10,6},{14,10},{7,3},{... | collective-permute-start | bytes 786440 | tf_op jit(solution)/shard_map/ppermute | solution.py:10
  17.5 1.3 %collective-permute-start.3 = (bf16[2048,64]{0,1:T(8,128)(2,1)S(1)}, bf16[2048,64]{0,1:T(8,128)(2,1)S(1)}, u32[]{:S(2)}, u32[]{:S(2)}) collective-permute-start(bf16[2048,64]{0,1:T(8,128)(2,1)S(1)} %all_gather.3), channel_id=1, source_target_pairs={{8,0},{12,4},{9,1},{13,5},{10,2},{14,6},{11,3},{15,7},{24,16},{28,... | collective-permute-start | bytes 786440 | tf_op jit(solution)/shard_map/ppermute | solution.py:10
  18.8 1.0 %fusion.34 = f32[64,64]{1,0:T(8,128)S(1)} fusion(bf16[512,64]{0,1:T(8,128)(2,1)} %param.17, bf16[512,64]{0,1:T(8,128)(2,1)S(1)} %convert_element_type.10), kind=kOutput, calls=%fused_computation.39 | convolution fusion | flops 4194304 | bytes 147456 | tf_op jit(solution)/shard_map/dot_general | solution.py:39
  19.8 11.4 %psum.7 = f32[64,64]{1,0:T(8,128)S(1)} all-reduce(f32[64,64]{1,0:T(8,128)S(1)} %fusion.34), channel_id=1, replica_groups=mesh['chain'=2,'cell'=4,'col'=4] {'col'}, use_global_device_ids=true, to_apply=%region_0.1 | all-reduce | flops 4096 | bytes 32768 | tf_op jit(solution)/shard_map/psum | solution.py:45
  31.2 0.8 %reshape.65 = f32[4,1,4096]{2,1,0:T(1,128)} reshape(f32[4,1,64,64]{3,2,1,0:T(8,128)S(1)} %stack.23) | data formatting | bytes 131072
  32.0 6.1 %all-to-all-start = ((f32[4,1,4096]{2,1,0:T(1,128)}), f32[4,1,4096]{2,1,0:T(1,128)S(1)}, u32[]{:S(2)}, u32[]{:S(2)}) async-start(f32[4,1,4096]{2,1,0:T(1,128)} %reshape.65), calls=%async_computation | async-start | bytes 131072 | tf_op jit(solution)/shard_map/all_to_all | solution.py:47
  38.1 1.3 %dynamic_slice.17 = s32[1]{0:T(128)} dynamic-slice(s32[4]{0:T(128)} %param.12, s32[]{:T(128)S(6)} %select_n.45), dynamic_slice_sizes={1} | dynamic-slice | bytes 12 | tf_op jit(solution)/shard_map/dynamic_slice | solution.py:30
  40.6 1.2 %dynamic_slice.16 = s32[1]{0:T(128)} dynamic-slice(s32[4]{0:T(128)} %param.11, s32[]{:T(128)S(6)} %select_n.45), dynamic_slice_sizes={1} | dynamic-slice | bytes 12 | tf_op jit(solution)/shard_map/dynamic_slice | solution.py:38
  42.4 1.2 %dynamic_slice.19 = s32[1]{0:T(128)} dynamic-slice(s32[4]{0:T(128)} %param.14, s32[]{:T(128)S(6)} %select_n.45), dynamic_slice_sizes={1} | dynamic-slice | bytes 12 | tf_op jit(solution)/shard_map/dynamic_slice | solution.py:43
  43.6 0.7 %fusion.30 = s32[8]{0:T(128)S(1)} fusion(s32[4,8]{1,0:T(4,128)} %param.13, s32[]{:T(128)S(6)} %select_n.45), kind=kLoop, calls=%fused_computation.34 | loop fusion | flops 24 | bytes 68 | tf_op jit(solution)/shard_map/jit(_take)/jit(_where)/select_n | solution.py:19
  44.3 1.3 %compare_and_fusion = (pred[8]{0:T(512)(128)(4,1)S(1)}, pred[8]{0:T(512)(128)(4,1)S(1)}) fusion(s32[4,8]{1,0:T(4,128)} %param.13, s32[]{:T(128)S(6)} %select_n.45, s32[]{:T(128)} %bitcast.10), kind=kLoop, calls=%fused_computation.31 | loop fusion | flops 56 | bytes 56 | tf_op jit(solution)/shard_map/jit(_take)/and | solution.py:19
  45.6 0.5 broadcast.46
  46.1 0.8 %reduce = f32[4,4096]{1,0:T(4,128)S(1)} reduce(f32[4,1,4096]{2,1,0:T(1,128)S(1)} %all-to-all-done, f32[]{:T(128)} %broadcast.46), dimensions={1}, to_apply=%all_to_all.3.reduce_sub_computation | reduce | bytes 131076 | tf_op jit(solution)/shard_map/all_to_all | solution.py:47
  46.9 0.1 reshape.66
  47.0 0.6 %gather_fusion = f32[8,64,64]{2,1,0:T(8,128)S(1)} fusion(f32[4,64,64]{2,1,0:T(8,128)S(1)} %bitcast.47, s32[1024]{0:T(1024)S(1)} %pad_clamp_fusion), kind=kCustom, calls=%fused_computation | custom fusion | bytes 262176 | tf_op jit(solution)/shard_map/jit(_take)/gather | solution.py:19
  47.6 0.0 copy-start.1
  47.6 1.6 %fusion.18 = bf16[64,64]{1,0:T(8,128)(2,1)S(1)} fusion(f32[1,8,64,64]{3,2,1,0:T(8,128)} %param.15, f32[8,64,64]{2,1,0:T(8,128)S(1)} %gather_fusion, pred[8]{0:T(512)(128)(4,1)S(1)} %get-tuple-element.5, pred[8]{0:T(512)(128)(4,1)S(1)} %get-tuple-element.6), kind=kOutput, calls=%fused_computation.13 | convolution fusion | flops 25235456 | bytes 270352 | tf_op jit(solution)/shard_map/kab,kbw->aw/dot_general | solution.py:22
  49.2 0.2 convolution_bitcast_fusion
  49.4 2.4 %fusion.15 = f32[512,64]{0,1:T(8,128)S(1)} fusion(bf16[1,2,512,2048]{3,2,1,0:T(8,128)(2,1)} %param.10, s32[]{:T(128)S(6)} %select_n.47, bf16[1,2048,64]{1,2,0:T(8,128)(2,1)S(1)} %bitcast.48, bf16[1,2048,64]{1,2,0:T(8,128)(2,1)S(1)} %bitcast.49, bf16[1,2048,64]{1,2,0:T(8,128)(2,1)S(1)} %bitcast.50, bf16[1,2048,64]{1,2,0:T(8,128)(2,1)S(1)} %bitcast.51, ...), kind=kOutput, calls=%fused_computation.10 | convolution fusion | flops 134643712 | bytes 3277316 | tf_op jit(solution)/shard_map/dot_general | solution.py:37
  51.8 1.4 %fusion.9 = f32[512,64]{0,1:T(8,128)} fusion(f32[512,64]{0,1:T(8,128)S(1)} %convolution_bitcast_fusion, f32[512,64]{0,1:T(8,128)S(1)} %fusion.15, bf16[2048,64]{0,1:T(8,128)(2,1)S(1)} %all_gather.3, bf16[1,2,512,2048]{3,2,1,0:T(8,128)(2,1)S(1)} %copy-done.1), kind=kOutput, calls=%fused_computation.8 | convolution fusion | flops 134283264 | bytes 2752512 | tf_op jit(solution)/shard_map/dot_general | solution.py:36
  (10 shorter events, 0.0 us)
Async XLA Ops:
  0.0 49.2 %copy-start = (bf16[512,64]{0,1:T(8,128)(2,1)S(1)}, bf16[512,64]{0,1:T(8,128)(2,1)}, u32[]{:S(2)}) copy-start(bf16[512,64]{0,1:T(8,128)(2,1)} %param.16) | copy-start | bytes 196612
  8.2 41.2 %collective-permute-start = (bf16[2048,64]{0,1:T(8,128)(2,1)S(1)}, bf16[2048,64]{0,1:T(8,128)(2,1)S(1)}, u32[]{:S(2)}, u32[]{:S(2)}) collective-permute-start(bf16[2048,64]{0,1:T(8,128)(2,1)S(1)} %all_gather.3), channel_id=1, source_target_pairs={{0,8},{4,12},{1,9},{5,13},{2,10},{6,14},{3,11},{7,15},{16,24},{20,... | collective-permute-start | bytes 786440 | tf_op jit(solution)/shard_map/ppermute | solution.py:10
  12.7 36.7 %collective-permute-start.1 = (bf16[2048,64]{0,1:T(8,128)(2,1)S(1)}, bf16[2048,64]{0,1:T(8,128)(2,1)S(1)}, u32[]{:S(2)}, u32[]{:S(2)}) collective-permute-start(bf16[2048,64]{0,1:T(8,128)(2,1)S(1)} %all_gather.3), channel_id=1, source_target_pairs={{0,4},{4,8},{8,12},{1,5},{5,9},{9,13},{2,6},{6,10},{10,14},{3,7},{... | collective-permute-start | bytes 786440 | tf_op jit(solution)/shard_map/ppermute | solution.py:10
  16.2 33.2 %collective-permute-start.2 = (bf16[2048,64]{0,1:T(8,128)(2,1)S(1)}, bf16[2048,64]{0,1:T(8,128)(2,1)S(1)}, u32[]{:S(2)}, u32[]{:S(2)}) collective-permute-start(bf16[2048,64]{0,1:T(8,128)(2,1)S(1)} %all_gather.3), channel_id=1, source_target_pairs={{4,0},{8,4},{12,8},{5,1},{9,5},{13,9},{6,2},{10,6},{14,10},{7,3},{... | collective-permute-start | bytes 786440 | tf_op jit(solution)/shard_map/ppermute | solution.py:10
  17.5 31.9 %collective-permute-start.3 = (bf16[2048,64]{0,1:T(8,128)(2,1)S(1)}, bf16[2048,64]{0,1:T(8,128)(2,1)S(1)}, u32[]{:S(2)}, u32[]{:S(2)}) collective-permute-start(bf16[2048,64]{0,1:T(8,128)(2,1)S(1)} %all_gather.3), channel_id=1, source_target_pairs={{8,0},{12,4},{9,1},{13,5},{10,2},{14,6},{11,3},{15,7},{24,16},{28,... | collective-permute-start | bytes 786440 | tf_op jit(solution)/shard_map/ppermute | solution.py:10
  32.0 13.6 %all-to-all-start = ((f32[4,1,4096]{2,1,0:T(1,128)}), f32[4,1,4096]{2,1,0:T(1,128)S(1)}, u32[]{:S(2)}, u32[]{:S(2)}) async-start(f32[4,1,4096]{2,1,0:T(1,128)} %reshape.65), calls=%async_computation | async-start | bytes 131072 | tf_op jit(solution)/shard_map/all_to_all | solution.py:47
  47.6 4.2 %copy-start.1 = (bf16[1,2,512,2048]{3,2,1,0:T(8,128)(2,1)S(1)}, bf16[1,2,512,2048]{3,2,1,0:T(8,128)(2,1)}, u32[]{:S(2)}) copy-start(bf16[1,2,512,2048]{3,2,1,0:T(8,128)(2,1)} %param.10) | copy-start | bytes 12582916
